TPU v7x, 256 devices: a whole 4x4x8 slice. The times are simulated.
256 devices in a mesh: seq: 64 (over y, z, x_hi), mp: 4 (over x_lo, core).
Axes of the slice: x: 4 (x_hi: 2, x_lo: 2; x = x_hi * 2 + x_lo), y: 4, z: 8, core: 2. Of those that a mesh axis runs over, the one named last changes fastest.
Arguments:
- stream: bfloat16 [20480, 1024], P('seq'), as said below
- gain_attn: float32 [1024], replicated, may hold values from 0.1 to 1.9
- gain_mlp: float32 [1024], replicated, may hold values from 0.1 to 1.9
- gain_read: float32 [1024], replicated, may hold values from 0.1 to 1.9
- query_weight: bfloat16 [1024, 1024], P(None, 'mp'), as said below
- key_weight: bfloat16 [1024, 1024], P(None, 'mp'), as said below
- value_weight: bfloat16 [1024, 1024], P(None, 'mp'), may hold values from -0.1875 to 0.1875
- out_weight: bfloat16 [1024, 1024], P('mp'), may hold values from -0.1875 to 0.1875
- up_weight: bfloat16 [1024, 2048], P(None, 'mp'), may hold values from -0.1875 to 0.1875
- down_weight: bfloat16 [2048, 1024], P('mp'), may hold values from -0.125 to 0.125
- read_weight: bfloat16 [1024, 8192], P(None, 'mp'), may hold values from -0.1875 to 0.1875
- read_bias: float32 [8192], P('mp'), may hold values from -3 to 3
- spike_counts: int32 [20480, 8192], P('seq', 'mp'), may hold values from 0 to 7
Outputs:
- log_rate: bfloat16 [20480, 8192], P('seq', 'mp')
- poisson_loss: float32 [20480], P('seq')
Inputs may be any that keep to these rules, and one draw needn't show every extreme that they name: Real-valued residual stream. `query_weight`: Real-valued projection. `key_weight`: Real-valued projection.
All inputs are finite; a program needn't handle non-finite values.
Results may differ from a plain program's by a relative error of at most 0.014.
Values may be sent and summed in bfloat16 or wider, within the bound.
A program may use at most 128 MiB of HBM per device.

v0:
```python
import jax
import jax.numpy as jnp
from jax import lax
from jax.sharding import PartitionSpec as P

DH = 64
NEU = 8192


def rms_norm(field, gain):
    wide = field.astype(jnp.float32)
    scale = lax.rsqrt(jnp.mean(wide * wide, axis=-1, keepdims=True) + 1e-05)
    return wide * scale * gain


def per_device(
    stream,
    gain_attn,
    gain_mlp,
    gain_read,
    query_weight,
    key_weight,
    value_weight,
    out_weight,
    up_weight,
    down_weight,
    read_weight,
    read_bias,
    spike_counts,
):
    shard_rows = stream.shape[0]
    my_index = lax.axis_index("seq")

    def position(device, within):
        return device * shard_rows + within

    normed = rms_norm(stream, gain_attn).astype(jnp.bfloat16)
    queries_flat = jnp.dot(normed, query_weight, preferred_element_type=jnp.float32).astype(
        jnp.bfloat16
    )
    keys_flat = jnp.dot(normed, key_weight, preferred_element_type=jnp.float32).astype(jnp.bfloat16)
    values_flat = jnp.dot(normed, value_weight, preferred_element_type=jnp.float32).astype(
        jnp.bfloat16
    )
    local_heads = queries_flat.shape[1] // DH
    factor = DH ** (-0.5)
    queries = queries_flat.reshape(shard_rows, local_heads, DH)
    query_pos = position(my_index, jnp.arange(shard_rows, dtype=jnp.int32))
    query_last = jnp.max(query_pos)
    init = (
        jnp.full((local_heads, shard_rows), -1e30, jnp.float32),
        jnp.zeros((local_heads, shard_rows), jnp.float32),
        jnp.zeros((local_heads, shard_rows, DH), jnp.float32),
    )
    state = init
    keys_piece = lax.all_gather(keys_flat, "seq", axis=0, tiled=True)
    values_piece = lax.all_gather(values_flat, "seq", axis=0, tiled=True)
    piece_rows = keys_piece.shape[0]
    gathered_rows = jnp.arange(piece_rows, dtype=jnp.int32)
    key_pos = position(gathered_rows // shard_rows, gathered_rows % shard_rows)
    block_rows = 512
    block_count = piece_rows // block_rows

    def one_block(inner_state, block_index):
        offset = block_index * block_rows
        key_block = lax.dynamic_slice_in_dim(keys_piece, offset, block_rows, 0).reshape(
            block_rows, local_heads, DH
        )
        value_block = lax.dynamic_slice_in_dim(values_piece, offset, block_rows, 0).reshape(
            block_rows, local_heads, DH
        )
        block_pos = lax.dynamic_slice_in_dim(key_pos, offset, block_rows, 0)

        def update(current):
            best, total_weight, accum = current
            scores = (
                jnp.einsum("qhd,khd->hqk", queries, key_block, preferred_element_type=jnp.float32)
                * factor
            )
            allowed = block_pos[None, None, :] <= query_pos[None, :, None]
            scores = jnp.where(allowed, scores, -1e30)
            fresh = jnp.maximum(best, jnp.max(scores, axis=-1))
            weights = jnp.where(allowed, jnp.exp(scores - fresh[..., None]), 0.0)
            decay = jnp.exp(best - fresh)
            total_weight = total_weight * decay + jnp.sum(weights, axis=-1)
            weights_low = weights.astype(jnp.bfloat16)
            accum = accum * decay[..., None] + jnp.einsum(
                "hqk,khd->hqd", weights_low, value_block, preferred_element_type=jnp.float32
            )
            return (fresh, total_weight, accum)

        def keep(current):
            return current

        return (lax.cond(jnp.min(block_pos) > query_last, keep, update, inner_state), None)

    state, unused = lax.scan(one_block, state, jnp.arange(block_count, dtype=jnp.int32))
    best, total_weight, accum = state
    attended = (
        jnp.transpose(accum / total_weight[..., None], (1, 0, 2))
        .reshape(shard_rows, local_heads * DH)
        .astype(jnp.bfloat16)
    )
    attn_part = jnp.dot(attended, out_weight, preferred_element_type=jnp.float32)
    attn_total = lax.psum(attn_part.astype(jnp.bfloat16), "mp").astype(jnp.float32)
    resid = (stream.astype(jnp.float32) + attn_total).astype(jnp.bfloat16)
    mlp_in = rms_norm(resid, gain_mlp).astype(jnp.bfloat16)
    hidden = jax.nn.gelu(
        jnp.dot(mlp_in, up_weight, preferred_element_type=jnp.float32), approximate=True
    ).astype(jnp.bfloat16)
    mlp_part = jnp.dot(hidden, down_weight, preferred_element_type=jnp.float32)
    outcome = resid.astype(jnp.float32) + lax.psum(mlp_part.astype(jnp.bfloat16), "mp").astype(
        jnp.float32
    )
    read_in = rms_norm(outcome, gain_read).astype(jnp.bfloat16)
    rate_full = jnp.dot(read_in, read_weight, preferred_element_type=jnp.float32) + read_bias
    loss_part = jnp.sum(jnp.exp(rate_full) - spike_counts.astype(jnp.float32) * rate_full, axis=-1)
    poisson_loss = lax.psum(loss_part, "mp") / NEU
    return (rate_full.astype(jnp.bfloat16), poisson_loss)


def solution(mesh):
    in_specs = (
        P("seq", None),
        P(),
        P(),
        P(),
        P(None, "mp"),
        P(None, "mp"),
        P(None, "mp"),
        P("mp", None),
        P(None, "mp"),
        P("mp", None),
        P(None, "mp"),
        P("mp"),
        P("seq", "mp"),
    )
    out_specs = (P("seq", "mp"), P("seq"))
    return jax.shard_map(
        per_device, mesh=mesh, in_specs=in_specs, out_specs=out_specs, check_vma=False
    )
```

profile of v0, /device:TPU:1, one launch (start us, length us, event | category | flops | bytes accessed | tf_op | source)
XLA Modules:
  0.0 773.9 jit_solution(6381487957085612974)
XLA Ops:
  7.3 1.5 fusion.14
  8.7 2.3 convolution_convert_fusion.4
  11.2 1.1 convolution_convert_fusion.2
  13.6 165.9 %all-gather.3.cloned.1.call-done = bf16[20480,256]{1,0:T(8,128)(2,1)} async-done(((bf16[320,256]{1,0:T(8,128)(2,1)}), bf16[20480,256]{1,0:T(8,128)(2,1)}) %all-gather.3.cloned.1.call-update) | async-done | bytes 10485776 | tf_op jit(solution)/shard_map/all_gather | solution.py:56
  179.5 14.2 %copy.19 = bf16[20480,256]{0,1:T(8,128)(2,1)} copy(bf16[20480,256]{1,0:T(8,128)(2,1)} %all-gather.3.cloned.1.call-done) | data formatting | bytes 20971520
  193.7 150.1 %all-gather.5.cloned.1.call-done = bf16[20480,256]{1,0:T(8,128)(2,1)} async-done(((bf16[320,256]{1,0:T(8,128)(2,1)}), bf16[20480,256]{1,0:T(8,128)(2,1)}) %all-gather.5.cloned.1.call-update) | async-done | bytes 10485776 | tf_op jit(solution)/shard_map/all_gather | solution.py:57
  343.8 14.2 %copy.20 = bf16[20480,256]{0,1:T(8,128)(2,1)} copy(bf16[20480,256]{1,0:T(8,128)(2,1)} %all-gather.5.cloned.1.call-done) | data formatting | bytes 20971520
  358.1 138.6 %while.15 = (s32[]{:T(128)}, f32[4,320]{1,0:T(4,128)S(1)}, f32[4,320]{1,0:T(4,128)S(1)}, f32[4,320,64]{1,2,0:T(8,128)S(1)}, s32[40]{0:T(128)S(1)}, /*index=5*/s3...) while((s32[]{:T(128)}, f32[4,320]{1,0:T(4,128)S(1)}, ...), condition=%wide.region_8.9_spmd.clone, body=%wide.region_2.8_spmd.clone.sunk | while | flops 176622912 | bytes 11005285 | solution.py:97
  359.4 0.7 fusion.75
  361.4 4.3 conditional.3
  361.6 1.3 constant_dynamic-slice_fusion
  363.0 0.7 fusion.2
  363.7 1.0 fusion.4
  364.7 1.0 fusion.8
  367.0 0.7 fusion.75
  370.4 0.7 fusion.75
  373.7 0.7 fusion.75
  377.1 0.7 fusion.75
  380.4 0.7 fusion.75
  383.8 0.7 fusion.75
  387.2 0.7 fusion.75
  390.5 0.7 fusion.75
  393.9 0.7 fusion.75
  397.2 0.7 fusion.75
  496.8 1.2 convolution_convert_fusion.1
  498.0 206.9 %all-reduce.3.cloned.1.call-done = bf16[320,1024]{1,0:T(8,128)(2,1)} async-done(((bf16[320,1024]{1,0:T(8,128)(2,1)}), bf16[320,1024]{1,0:T(8,128)(2,1)}) %all-reduce.3.cloned.1.call-update) | async-done | bytes 655376 | tf_op jit(solution)/shard_map/psum | solution.py:105
  705.0 1.4 fusion.18
  706.4 3.1 convolution_convert_fusion
  709.6 44.4 %all-reduce.5.cloned.1.call-done = bf16[320,1024]{1,0:T(8,128)(2,1)} async-done(((bf16[320,1024]{1,0:T(8,128)(2,1)}), bf16[320,1024]{1,0:T(8,128)(2,1)}) %all-reduce.5.cloned.1.call-update) | async-done | bytes 655376 | tf_op jit(solution)/shard_map/psum | solution.py:112
  754.0 1.4 multiply_reduce_fusion
  755.4 6.2 subtract_reduce_fusion
  761.6 5.1 psum.23
  (270 shorter events, 48.9 us)
Async XLA Ops:
  7.2 699.2 %copy-start = (bf16[512,1024]{1,0:T(8,128)(2,1)S(1)}, bf16[512,1024]{1,0:T(8,128)(2,1)}, u32[]{:S(2)}) copy-start(bf16[512,1024]{1,0:T(8,128)(2,1)} %param.26) | copy-start | bytes 3145732
  7.2 4.0 copy-start.1
  7.2 4.0 copy-start.6
  7.2 4.0 copy-start.3
  7.2 5.1 copy-start.4
  7.2 172.3 %all-gather.3.cloned.1.call-start = ((), (), s32[]{:S(2)}) async-start(), calls=%async_computation | async-start | bytes 10649600 | tf_op jit(solution)/shard_map/all_gather | solution.py:56
  11.1 332.7 %all-gather.5.cloned.1.call-start = ((), (), s32[]{:S(2)}) async-start(), calls=%async_computation.1 | async-start | bytes 10649600 | tf_op jit(solution)/shard_map/all_gather | solution.py:57
  12.2 692.7 %all-reduce.3.cloned.1.call-start = ((), (), s32[]{:S(2)}) async-start(), calls=%async_computation.2 | async-start | bytes 1310720 | tf_op jit(solution)/shard_map/psum | solution.py:105
  358.1 138.7 %copy-start.2 = (bf16[256,1024]{1,0:T(8,128)(2,1)S(1)}, bf16[256,1024]{1,0:T(8,128)(2,1)}, u32[]{:S(2)}) copy-start(bf16[256,1024]{1,0:T(8,128)(2,1)} %param.24) | copy-start | bytes 1572868
  496.7 209.7 %copy-start.7 = (f32[1024]{0:T(1024)S(1)}, f32[1024]{0:T(1024)}, u32[]{:S(2)}) copy-start(f32[1024]{0:T(1024)} %param.19) | copy-start | bytes 12292
  498.0 256.0 %all-reduce.5.cloned.1.call-start = ((), (), s32[]{:S(2)}) async-start(), calls=%async_computation.3 | async-start | bytes 1310720 | tf_op jit(solution)/shard_map/psum | solution.py:112
  706.4 49.0 %copy-start.5 = (f32[2048]{0:T(1024)S(1)}, f32[2048]{0:T(1024)}, u32[]{:S(2)}) copy-start(f32[2048]{0:T(1024)} %param.28) | copy-start | bytes 24580
  706.4 49.0 %copy-start.8 = (f32[1024]{0:T(1024)S(1)}, f32[1024]{0:T(1024)}, u32[]{:S(2)}) copy-start(f32[1024]{0:T(1024)} %param.20) | copy-start | bytes 12292
Sparse Core Ops, SparseCore 0:
  12.1 167.3 all-gather.2
  183.0 160.7 all-gather.4
  498.1 206.7 all-reduce.2
  709.7 44.2 all-reduce.4
where the time goes:
time: 777 us; the launch traced here: 774 us
  waiting for transfers between devices  567 us (73%)
  loops' own time  81 us (10%)
  local copies, waits for them, and re-layouts  53.8 us (7%)
  other arithmetic  36.5 us (5%)
  matrix products  16 us (2%)
  between operations  14 us (2%)
    psum x1, waiting for transfers between devices, per_device(): lax.psum(attn_part.astype(jnp.bfloat16), 'mp').astype(jnp.float32)  207 us
    all_gather x1, waiting for transfers between devices, per_device(): keys_piece = lax.all_gather(keys_flat, 'seq', axis=0, tiled=True)  166 us
    all_gather x1, waiting for transfers between devices, per_device(): values_piece = lax.all_gather(values_flat, 'seq', axis=0, tiled=True)  150 us
    another operation x1, loops' own time, per_device(): lax.scan(one_block, state, jnp.arange(block_count, dtype=jnp.int32))  79.8 us
    psum x1, waiting for transfers between devices, per_device(): lax.psum(mlp_part.astype(jnp.bfloat16), 'mp').astype(jnp.float32)  44.4 us
    reduce_min x40, other arithmetic, one_block(): jnp.min(block_pos) > query_last  29.6 us
    unnamed x20, local copies, waits for them, and re-layouts  28.5 us
    dynamic_slice x40, local copies, waits for them, and re-layouts, per_device(): lax.scan(one_block, state, jnp.arange(block_count, dtype=jnp.int32))  23.5 us
  transfers between devices with their start and end apart: 4, of which 4 were waited for; matrix products, arithmetic and copies ran while one was open for 2% of the time, Pallas kernels for 0%

commit v1 on v0

--- a/solution.py
+++ b/solution.py
@@ -54,7 +54,9 @@
     )
     state = init
     keys_piece = lax.all_gather(keys_flat, "seq", axis=0, tiled=True)
-    values_piece = lax.all_gather(values_flat, "seq", axis=0, tiled=True)
+    values_piece = jnp.concatenate(
+        lax.all_to_all(jnp.stack([values_flat] * lax.axis_size("seq")), "seq", 0, 0), axis=0
+    )
     piece_rows = keys_piece.shape[0]
     gathered_rows = jnp.arange(piece_rows, dtype=jnp.int32)
     key_pos = position(gathered_rows // shard_rows, gathered_rows % shard_rows)

time: 777 us -> 751 us (0.967)
  waiting for transfers between devices: 567 us -> 524 us
  starting transfers between devices: 0.16 us -> 15.6 us
    all_to_all x0 -> x1, waiting for transfers between devices: none -> 271 us  [per_device(): lax.all_to_all(jnp.stack([values_flat] * lax.axis_size('seq')), 'seq', 0, 0)]
    all_gather x1, waiting for transfers between devices: 166 us -> 0.01 us  [per_device(): keys_piece = lax.all_gather(keys_flat, 'seq', axis=0, tiled=True)]
    all_gather x1 -> x0, waiting for transfers between devices: 150 us -> none  [per_device(): values_piece = lax.all_gather(values_flat, 'seq', axis=0, tiled=True)]
    all_to_all x0 -> x1, starting transfers between devices: none -> 15.5 us  [per_device(): lax.all_to_all(jnp.stack([values_flat] * lax.axis_size('seq')), 'seq', 0, 0)]
  transfers between devices with their start and end apart: 4 -> 4, of which waited for: 4 -> 3; matrix products, arithmetic and copies ran while one was open for 2% -> 2% of each run, Pallas kernels for 0% -> 0%
where the time goes in v1:
time: 751 us; the launch traced here: 748 us
  waiting for transfers between devices  524 us (70%)
  loops' own time  78.7 us (10%)
  local copies, waits for them, and re-layouts  59.1 us (8%)
  other arithmetic  36.4 us (5%)
  starting transfers between devices  15.6 us (2%)
  matrix products  15.3 us (2%)
  between operations  13.9 us (2%)
    all_to_all x1, waiting for transfers between devices, per_device(): lax.all_to_all(jnp.stack([values_flat] * lax.axis_size('seq')), 'seq', 0, 0)  271 us
    psum x1, waiting for transfers between devices, per_device(): lax.psum(attn_part.astype(jnp.bfloat16), 'mp').astype(jnp.float32)  209 us
    another operation x1, loops' own time, per_device(): lax.scan(one_block, state, jnp.arange(block_count, dtype=jnp.int32))  77.6 us
    psum x1, waiting for transfers between devices, per_device(): lax.psum(mlp_part.astype(jnp.bfloat16), 'mp').astype(jnp.float32)  44.4 us
    reduce_min x40, other arithmetic, one_block(): jnp.min(block_pos) > query_last  29.6 us
    unnamed x20, local copies, waits for them, and re-layouts  28.6 us
    dynamic_slice x40, local copies, waits for them, and re-layouts, per_device(): lax.scan(one_block, state, jnp.arange(block_count, dtype=jnp.int32))  23.5 us
    all_to_all x1, starting transfers between devices, per_device(): lax.all_to_all(jnp.stack([values_flat] * lax.axis_size('seq')), 'seq', 0, 0)  15.5 us
  transfers between devices with their start and end apart: 4, of which 3 were waited for; matrix products, arithmetic and copies ran while one was open for 2% of the time, Pallas kernels for 0%

profile of v1, /device:TPU:1, one launch (start us, length us, event | category | flops | bytes accessed | tf_op | source)
XLA Modules:
  0.0 748.0 jit_solution(16132447292197089451)
XLA Ops:
  7.2 1.4 fusion.14
  8.6 1.6 convolution_convert_fusion.2
  10.2 5.3 stack.2
  15.5 15.5 %all-to-all-start = ((bf16[64,320,256]{2,1,0:T(8,128)(2,1)}), bf16[64,320,256]{2,1,0:T(8,128)(2,1)}, u32[]{:S(2)}, u32[]{:S(2)}) async-start(bf16[64,320,256]{2,1,0:T(8,128)(2,1)} %stack.2), calls=%async_computation | async-start | bytes 20971520 | tf_op jit(solution)/shard_map/all_to_all | solution.py:58
  31.1 1.1 convolution_convert_fusion.4
  33.5 270.6 %all-to-all-done = bf16[64,320,256]{2,1,0:T(8,128)(2,1)} async-done(((bf16[64,320,256]{2,1,0:T(8,128)(2,1)}), bf16[64,320,256]{2,1,0:T(8,128)(2,1)}, u32[]{:S(2)}, u32[]{:S(2)}) %all-to-all-start) | async-done | bytes 10485792 | tf_op jit(solution)/shard_map/all_to_all | solution.py:58
  304.1 14.3 %copy.20 = bf16[20480,256]{0,1:T(8,128)(2,1)} copy(bf16[20480,256]{1,0:T(8,128)(2,1)} %bitcast.4) | data formatting | bytes 20971520
  318.4 14.2 %copy.19 = bf16[20480,256]{0,1:T(8,128)(2,1)} copy(bf16[20480,256]{1,0:T(8,128)(2,1)} %all-gather.2.cloned.1.call-done) | data formatting | bytes 20971520
  332.7 136.3 %while.15 = (s32[]{:T(128)}, f32[4,320]{1,0:T(4,128)S(1)}, f32[4,320]{1,0:T(4,128)S(1)}, f32[4,320,64]{1,2,0:T(8,128)S(1)}, s32[40]{0:T(128)S(1)}, /*index=5*/s3...) while((s32[]{:T(128)}, f32[4,320]{1,0:T(4,128)S(1)}, ...), condition=%wide.region_8.9_spmd.clone, body=%wide.region_2.8_spmd.clone.sunk | while | flops 176622912 | bytes 11005285 | solution.py:99
  334.0 0.7 fusion.75
  336.0 4.3 conditional.3
  336.2 1.3 constant_dynamic-slice_fusion
  337.5 0.7 fusion.2
  338.3 1.0 fusion.4
  339.3 1.0 fusion.8
  341.6 0.7 fusion.75
  344.9 0.7 fusion.75
  348.2 0.7 fusion.75
  351.5 0.7 fusion.75
  354.8 0.7 fusion.75
  358.1 0.7 fusion.75
  361.4 0.7 fusion.75
  364.7 0.7 fusion.75
  368.0 0.7 fusion.75
  469.1 1.2 convolution_convert_fusion.1
  470.4 208.7 %all-reduce.3.cloned.1.call-done = bf16[320,1024]{1,0:T(8,128)(2,1)} async-done(((bf16[320,1024]{1,0:T(8,128)(2,1)}), bf16[320,1024]{1,0:T(8,128)(2,1)}) %all-reduce.3.cloned.1.call-update) | async-done | bytes 655376 | tf_op jit(solution)/shard_map/psum | solution.py:107
  679.1 1.4 fusion.18
  680.5 3.1 convolution_convert_fusion
  683.7 44.4 %all-reduce.5.cloned.1.call-done = bf16[320,1024]{1,0:T(8,128)(2,1)} async-done(((bf16[320,1024]{1,0:T(8,128)(2,1)}), bf16[320,1024]{1,0:T(8,128)(2,1)}) %all-reduce.5.cloned.1.call-update) | async-done | bytes 655376 | tf_op jit(solution)/shard_map/psum | solution.py:114
  728.1 1.4 multiply_reduce_fusion
  729.5 6.2 subtract_reduce_fusion
  735.7 5.2 psum.23
  (270 shorter events, 49.5 us)
Async XLA Ops:
  7.2 673.3 %copy-start = (bf16[512,1024]{1,0:T(8,128)(2,1)S(1)}, bf16[512,1024]{1,0:T(8,128)(2,1)}, u32[]{:S(2)}) copy-start(bf16[512,1024]{1,0:T(8,128)(2,1)} %param.26) | copy-start | bytes 3145732
  15.5 15.6 %copy-start.1 = (bf16[320,1024]{1,0:T(8,128)(2,1)S(1)}, bf16[320,1024]{1,0:T(8,128)(2,1)}, u32[]{:S(2)}) copy-start(bf16[320,1024]{1,0:T(8,128)(2,1)} %param.17) | copy-start | bytes 1966084
  15.5 15.6 %copy-start.3 = (bf16[1024,256]{1,0:T(8,128)(2,1)S(1)}, bf16[1024,256]{1,0:T(8,128)(2,1)}, u32[]{:S(2)}) copy-start(bf16[1024,256]{1,0:T(8,128)(2,1)} %param.22) | copy-start | bytes 1572868
  15.5 15.6 %copy-start.6 = (f32[1024]{0:T(1024)S(1)}, f32[1024]{0:T(1024)}, u32[]{:S(2)}) copy-start(f32[1024]{0:T(1024)} %param.18) | copy-start | bytes 12292
  15.5 16.7 %copy-start.4 = (bf16[1024,256]{1,0:T(8,128)(2,1)S(1)}, bf16[1024,256]{1,0:T(8,128)(2,1)}, u32[]{:S(2)}) copy-start(bf16[1024,256]{1,0:T(8,128)(2,1)} %param.21) | copy-start | bytes 1572868
  15.5 288.6 %all-to-all-start = ((bf16[64,320,256]{2,1,0:T(8,128)(2,1)}), bf16[64,320,256]{2,1,0:T(8,128)(2,1)}, u32[]{:S(2)}, u32[]{:S(2)}) async-start(bf16[64,320,256]{2,1,0:T(8,128)(2,1)} %stack.2), calls=%async_computation | async-start | bytes 20971520 | tf_op jit(solution)/shard_map/all_to_all | solution.py:58
  31.0 287.4 %all-gather.2.cloned.1.call-start = ((), (), s32[]{:S(2)}) async-start(), calls=%async_computation.1 | async-start | bytes 10649600 | tf_op jit(solution)/shard_map/all_gather | solution.py:56
  32.2 646.9 %all-reduce.3.cloned.1.call-start = ((), (), s32[]{:S(2)}) async-start(), calls=%async_computation.2 | async-start | bytes 1310720 | tf_op jit(solution)/shard_map/psum | solution.py:107
  332.7 136.4 %copy-start.2 = (bf16[256,1024]{1,0:T(8,128)(2,1)S(1)}, bf16[256,1024]{1,0:T(8,128)(2,1)}, u32[]{:S(2)}) copy-start(bf16[256,1024]{1,0:T(8,128)(2,1)} %param.24) | copy-start | bytes 1572868
  469.0 211.5 %copy-start.7 = (f32[1024]{0:T(1024)S(1)}, f32[1024]{0:T(1024)}, u32[]{:S(2)}) copy-start(f32[1024]{0:T(1024)} %param.19) | copy-start | bytes 12292
  470.3 257.8 %all-reduce.5.cloned.1.call-start = ((), (), s32[]{:S(2)}) async-start(), calls=%async_computation.3 | async-start | bytes 1310720 | tf_op jit(solution)/shard_map/psum | solution.py:114
  680.5 49.0 %copy-start.5 = (f32[2048]{0:T(1024)S(1)}, f32[2048]{0:T(1024)}, u32[]{:S(2)}) copy-start(f32[2048]{0:T(1024)} %param.28) | copy-start | bytes 24580
  680.5 49.0 %copy-start.8 = (f32[1024]{0:T(1024)S(1)}, f32[1024]{0:T(1024)}, u32[]{:S(2)}) copy-start(f32[1024]{0:T(1024)} %param.20) | copy-start | bytes 12292
Sparse Core Ops, SparseCore 0:
  35.9 277.4 all-gather.1
  470.5 208.5 all-reduce.2
  683.8 44.2 all-reduce.4
